TPU v7x, 32 devices: a whole 2x2x4 slice. The times are simulated.
32 devices in a mesh: wide: 8 (over y, x, core), narrow: 4 (over z).
Axes of the slice: x: 2, y: 2, z: 4, core: 2. Of those that a mesh axis runs over, the one named last changes fastest.
Arguments:
- events: bfloat16 [8192, 1024], P('wide'), may hold values from -36 to 36
- lengths: int32 [24], replicated, may hold values from 1 to 2048, 8192 in all
- in_gain: float32 [1024], replicated, may hold values from 0.1 to 1.9
- w_uvqk: bfloat16 [1024, 8, 512], P(None, 'narrow'), may hold values from -2 to 2, as said below
- out_gain: float32 [8, 128], P('narrow'), may hold values from 0.1 to 1.9
- w_out: bfloat16 [8, 128, 1024], P('narrow'), may hold values from -0.25 to 0.25
Outputs:
- layer_out: bfloat16 [8192, 1024], P('wide', 'narrow')
Inputs may be any that keep to these rules, and one draw needn't show every extreme that they name: `w_uvqk`: projection weights.
All inputs are finite; a program needn't handle non-finite values.
Results may differ from a plain program's by a relative error of at most 0.0036.
Values may be sent and summed in bfloat16 or wider, within the bound.
A program may use at most 64 MiB of HBM per device.

v0:
```python
import jax
import jax.numpy as jnp
from jax import lax
from jax.sharding import PartitionSpec as P


def from_behind(value, axis, steps):
    count = lax.axis_size(axis)
    initial, last = (max(0, -steps), min(count, count - steps))
    return lax.ppermute(value, axis, [(source, source + steps) for source in range(initial, last)])


def fetch_relay(pair):
    return from_behind((pair[0], pair[1]), "wide", 1)


def on_device(events, lengths, in_gain, w_uvqk, out_gain, w_out):
    rows_w = events.shape[0]
    heads_local = w_uvqk.shape[1]
    head_size = out_gain.shape[1]
    events_f = events.astype(jnp.float32)
    average = jnp.mean(events_f, axis=-1, keepdims=True)
    variance = jnp.mean((events_f - average) ** 2, axis=-1, keepdims=True)
    normed = ((events_f - average) * lax.rsqrt(variance + 1e-05) * in_gain).astype(jnp.bfloat16)
    projected = jnp.einsum("rd,dhc->rhc", normed, w_uvqk, preferred_element_type=jnp.float32)
    projected = jax.nn.silu(projected).astype(jnp.bfloat16)
    update_gate = projected[:, :, :head_size]
    values_own = projected[:, :, head_size : 2 * head_size]
    queries = projected[:, :, 2 * head_size : 3 * head_size]
    keys_own = projected[:, :, 3 * head_size :]
    user_ends = jnp.cumsum(lengths)

    def owner_of(grow):
        return jnp.sum((user_ends[None, :] <= grow[:, None]).astype(jnp.int32), axis=1)

    first_row = lax.axis_index("wide") * rows_w
    query_pos = first_row + jnp.arange(rows_w, dtype=jnp.int32)
    query_user = owner_of(query_pos)
    scaling = head_size ** (-0.5)

    def attend(running, key_rows, value_rows, key_first):
        key_count = key_rows.shape[0]
        block_rows = 512

        def block_step(carry, block_index):
            key_start = block_index * block_rows
            key_block = lax.dynamic_slice_in_dim(key_rows, key_start, block_rows, 0)
            value_block = lax.dynamic_slice_in_dim(value_rows, key_start, block_rows, 0)
            key_pos = key_first + key_start + jnp.arange(block_rows, dtype=jnp.int32)
            key_user = owner_of(key_pos)
            allowed = (
                (key_user[None, :] == query_user[:, None])
                & (key_pos[None, :] <= query_pos[:, None])
                & (key_pos[None, :] >= 0)
            )
            scores = (
                jnp.einsum("rhc,khc->hrk", queries, key_block, preferred_element_type=jnp.float32)
                * scaling
            )
            weights = jnp.where(allowed[None], jax.nn.silu(scores), 0.0).astype(jnp.bfloat16)
            carry = carry + jnp.einsum(
                "hrk,khc->rhc", weights, value_block, preferred_element_type=jnp.float32
            )
            return (carry, None)

        running, _ = lax.scan(
            block_step, running, jnp.arange(key_count // block_rows, dtype=jnp.int32)
        )
        return running

    attended = attend(
        jnp.zeros((rows_w, heads_local, head_size), jnp.float32), keys_own, values_own, first_row
    )
    reach = lax.axis_size("wide") // 4

    def relay_turn(turn_index, carry):
        keys_held, values_held, running = carry
        keys_held, values_held = fetch_relay((keys_held, values_held))
        running = attend(running, keys_held, values_held, first_row - turn_index * rows_w)
        return (keys_held, values_held, running)

    _, _, attended = lax.fori_loop(1, reach + 1, relay_turn, (keys_own, values_own, attended))
    centre = jnp.mean(attended, axis=-1, keepdims=True)
    deviation = jnp.mean((attended - centre) ** 2, axis=-1, keepdims=True)
    gated = (
        (attended - centre)
        * lax.rsqrt(deviation + 1e-05)
        * out_gain[None]
        * update_gate.astype(jnp.float32)
    )
    gated = gated.astype(jnp.bfloat16)
    columns = lax.all_to_all(w_out, "narrow", split_axis=2, concat_axis=0, tiled=True)
    summed = jnp.einsum(
        "rhc,hcd->rd",
        lax.all_gather(gated, "narrow", axis=1, tiled=True),
        columns,
        preferred_element_type=jnp.float32,
    )
    share = summed.shape[1]
    own_cols = lax.dynamic_slice_in_dim(events_f, lax.axis_index("narrow") * share, share, 1)
    return (own_cols + summed).astype(jnp.bfloat16)


def solution(mesh):
    in_specs = (
        P("wide", None),
        P(),
        P(),
        P(None, "narrow", None),
        P("narrow", None),
        P("narrow", None, None),
    )
    out_specs = P("wide", "narrow")
    return jax.shard_map(
        on_device, mesh=mesh, in_specs=in_specs, out_specs=out_specs, check_vma=False
    )
```

profile of v0, /device:TPU:3, one launch (start us, length us, event | category | flops | bytes accessed | tf_op | source)
XLA Modules:
  0.0 165.2 jit_solution(15008756031488288233)
XLA Ops:
  6.6 2.1 %convert_reduce_fusion.2 = f32[1024]{0:T(1024)S(1)} fusion(bf16[1024,1024]{1,0:T(8,128)(2,1)} %param.12), kind=kLoop, calls=%fused_computation.47 | loop fusion | flops 2096128 | bytes 2101248 | tf_op jit(solution)/shard_map/reduce_sum | solution.py:22
  8.6 2.3 %multiply_reduce_fusion = f32[1024]{0:T(1024)S(1)} fusion(bf16[1024,1024]{1,0:T(8,128)(2,1)} %param.12, f32[1024]{0:T(1024)S(1)} %broadcast_multiply_fusion.1), kind=kLoop, calls=%fused_computation.46 | loop fusion | flops 4193280 | bytes 2105344 | tf_op jit(solution)/shard_map/reduce_sum | solution.py:23
  11.0 3.4 %multiply_convert_fusion = bf16[1024,2,512]{2,0,1:T(8,128)(2,1)S(1)} fusion(bf16[1024,2,512]{2,1,0:T(2,128)(2,1)S(1)} %copy-done, bf16[1024,1024]{1,0:T(8,128)(2,1)S(1)} %copy-done.1, f32[1024]{0:T(1024)S(1)} %copy-done.5, f32[1024]{0:T(1024)S(1)} %add_rsqrt_fusion.1, f32[1024]{0:T(1024)S(1)} %broadcast_multiply_fusion.1), kind=kOutput, calls=%fused_computation.44 | convolution fusion | flops 2157969408 | bytes 6303744 | tf_op jit(solution)/shard_map/rd,dhc->rhc/dot_general | solution.py:25
  14.4 1.3 copy-done.2
  15.7 1.2 fusion.49
  17.6 12.9 %while.56 = (s32[]{:T(128)}, f32[1024,2,128]{0,2,1:T(8,128)}, s32[2]{0:T(128)S(1)}, bf16[1024,2,128]{0,2,1:T(8,128)(2,1)S(1)}, s32[24]{0:T(128)S(1)}, /*index=5*...) while((s32[]{:T(128)}, f32[1024,2,128]{0,2,1:T(8,128)}, ...), condition=%wide.region_6.7_spmd.clone.clone.clone, body=%wide.region_4.6_spmd.clone.clone.clone.sunk | while | flops 546871296 | bytes 4219704 | solution.py:66
  19.6 4.2 %fusion.65 = f32[1024,2,128]{0,2,1:T(8,128)} fusion(bf16[1024,2,128]{2,0,1:T(8,128)(2,1)} %get-tuple-element.781, pred[1024,512]{0,1:T(8,128)(4,1)S(1)} %and_and_fusion.4, f32[1024,2,128]{0,2,1:T(8,128)} %get-tuple-element.761, pred[]{:T(512)S(6)} %compare.5, bf16[1024,2,128]{2,0,1:T(8,128)(2,1)} %get-tuple-element.780, s32[]{:T(128)S(6)} %select_n.48, ...), kind=kOutput, calls=%fused_computation.33.clone.1 | convolution fusion | flops 544735232 | bytes 3671552 | tf_op jit(solution)/shard_map/while/body/eval_jaxpr/hrk,khc->rhc/dot_general | solution.py:61
  25.9 4.6 %fusion.65 = f32[1024,2,128]{0,2,1:T(8,128)} fusion(bf16[1024,2,128]{2,0,1:T(8,128)(2,1)} %get-tuple-element.781, pred[1024,512]{0,1:T(8,128)(4,1)S(1)} %and_and_fusion.4, f32[1024,2,128]{0,2,1:T(8,128)} %get-tuple-element.761, pred[]{:T(512)S(6)} %compare.5, bf16[1024,2,128]{2,0,1:T(8,128)(2,1)} %get-tuple-element.780, s32[]{:T(128)S(6)} %select_n.48, ...), kind=kOutput, calls=%fused_computation.33.clone.1 | convolution fusion | flops 544735232 | bytes 3671552 | tf_op jit(solution)/shard_map/while/body/eval_jaxpr/hrk,khc->rhc/dot_general | solution.py:61
  30.5 62.6 %while.55 = (s32[]{:T(128)}, bf16[1024,2,128]{2,0,1:T(8,128)(2,1)}, bf16[1024,2,128]{0,2,1:T(8,128)(2,1)S(1)}, f32[1024,2,128]{0,2,1:T(8,128)}, s32[]{:T(128)}, ...) while((s32[]{:T(128)}, bf16[1024,2,128]{2,0,1:T(8,128)(2,1)}, ...), condition=%wide.region_11.12_spmd.clone.clone, body=%wide.region_7.11_spmd.clone.clone.sunk | while | flops 546609152 | bytes 10511020 | solution.py:82
  30.5 3.7 %collective-permute-start = (bf16[1024,2,128]{2,0,1:T(8,128)(2,1)}, bf16[1024,2,128]{2,0,1:T(8,128)(2,1)S(1)}, u32[]{:S(2)}, u32[]{:S(2)}) collective-permute-start(bf16[1024,2,128]{2,0,1:T(8,128)(2,1)} %get-tuple-element.802), channel_id=1, source_target_pairs={{0,4},{4,8},{8,12},{12,16},{16,20},{20,24},{24,28},{1,5},{5,9},{9,... | collective-permute-start | bytes 1572872 | tf_op jit(solution)/shard_map/while/body/eval_jaxpr/ppermute | solution.py:10
  34.2 1.9 %collective-permute-start.1 = (bf16[1024,2,128]{0,2,1:T(8,128)(2,1)S(1)}, bf16[1024,2,128]{0,2,1:T(8,128)(2,1)}, u32[]{:S(2)}, u32[]{:S(2)}) collective-permute-start(bf16[1024,2,128]{0,2,1:T(8,128)(2,1)S(1)} %get-tuple-element.803), channel_id=1, source_target_pairs={{0,4},{4,8},{8,12},{12,16},{16,20},{20,24},{24,28},{1,5},{5,9},{9,... | collective-permute-start | bytes 1572872 | tf_op jit(solution)/shard_map/while/body/eval_jaxpr/ppermute | solution.py:10
  36.1 4.5 %collective-permute-done = bf16[1024,2,128]{2,0,1:T(8,128)(2,1)S(1)} collective-permute-done((bf16[1024,2,128]{2,0,1:T(8,128)(2,1)}, bf16[1024,2,128]{2,0,1:T(8,128)(2,1)S(1)}, u32[]{:S(2)}, u32[]{:S(2)}) %collective-permute-start) | collective-permute-done | bytes 524320 | tf_op jit(solution)/shard_map/while/body/eval_jaxpr/ppermute | solution.py:10
  40.6 5.5 %collective-permute-done.1 = bf16[1024,2,128]{0,2,1:T(8,128)(2,1)} collective-permute-done((bf16[1024,2,128]{0,2,1:T(8,128)(2,1)S(1)}, bf16[1024,2,128]{0,2,1:T(8,128)(2,1)}, u32[]{:S(2)}, u32[]{:S(2)}) %collective-permute-start.1) | collective-permute-done | bytes 524320 | tf_op jit(solution)/shard_map/while/body/eval_jaxpr/ppermute | solution.py:10
  46.1 13.0 %while.57 = (s32[]{:T(128)}, f32[1024,2,128]{0,2,1:T(8,128)}, s32[2]{0:T(128)S(1)}, bf16[1024,2,128]{0,2,1:T(8,128)(2,1)}, s32[24]{0:T(128)S(1)}, /*index=5*/s32...) while((s32[]{:T(128)}, f32[1024,2,128]{0,2,1:T(8,128)}, ...), condition=%wide.region_10.10_spmd, body=%wide.region_8.9_spmd.sunk | while | flops 546608128 | bytes 4215091 | solution.py:66
  48.0 4.6 %fusion.69 = f32[1024,2,128]{0,2,1:T(8,128)} fusion(f32[1024,2,128]{0,2,1:T(8,128)} %get-tuple-element.720, bf16[1024,2,128]{2,0,1:T(8,128)(2,1)} %get-tuple-element.742, pred[1024,512]{0,1:T(8,128)(4,1)S(1)} %and_and_fusion.5, bf16[1024,2,128]{2,0,1:T(8,128)(2,1)S(1)} %get-tuple-element.741, s32[]{:T(128)S(6)} %select_n.50, ...), kind=kOutput, calls=%fused_computation.12.clone.1 | convolution fusion | flops 544473088 | bytes 3671040 | tf_op jit(solution)/shard_map/while/body/eval_jaxpr/while/body/eval_jaxpr/hrk,khc->rhc/dot_general | solution.py:61
  54.5 4.6 %fusion.69 = f32[1024,2,128]{0,2,1:T(8,128)} fusion(f32[1024,2,128]{0,2,1:T(8,128)} %get-tuple-element.720, bf16[1024,2,128]{2,0,1:T(8,128)(2,1)} %get-tuple-element.742, pred[1024,512]{0,1:T(8,128)(4,1)S(1)} %and_and_fusion.5, bf16[1024,2,128]{2,0,1:T(8,128)(2,1)S(1)} %get-tuple-element.741, s32[]{:T(128)S(6)} %select_n.50, ...), kind=kOutput, calls=%fused_computation.12.clone.1 | convolution fusion | flops 544473088 | bytes 3671040 | tf_op jit(solution)/shard_map/while/body/eval_jaxpr/while/body/eval_jaxpr/hrk,khc->rhc/dot_general | solution.py:61
  60.9 5.4 %collective-permute-start = (bf16[1024,2,128]{2,0,1:T(8,128)(2,1)}, bf16[1024,2,128]{2,0,1:T(8,128)(2,1)S(1)}, u32[]{:S(2)}, u32[]{:S(2)}) collective-permute-start(bf16[1024,2,128]{2,0,1:T(8,128)(2,1)} %get-tuple-element.802), channel_id=1, source_target_pairs={{0,4},{4,8},{8,12},{12,16},{16,20},{20,24},{24,28},{1,5},{5,9},{9,... | collective-permute-start | bytes 1572872 | tf_op jit(solution)/shard_map/while/body/eval_jaxpr/ppermute | solution.py:10
  66.3 1.9 %collective-permute-start.1 = (bf16[1024,2,128]{0,2,1:T(8,128)(2,1)S(1)}, bf16[1024,2,128]{0,2,1:T(8,128)(2,1)}, u32[]{:S(2)}, u32[]{:S(2)}) collective-permute-start(bf16[1024,2,128]{0,2,1:T(8,128)(2,1)S(1)} %get-tuple-element.803), channel_id=1, source_target_pairs={{0,4},{4,8},{8,12},{12,16},{16,20},{20,24},{24,28},{1,5},{5,9},{9,... | collective-permute-start | bytes 1572872 | tf_op jit(solution)/shard_map/while/body/eval_jaxpr/ppermute | solution.py:10
  68.3 4.5 %collective-permute-done = bf16[1024,2,128]{2,0,1:T(8,128)(2,1)S(1)} collective-permute-done((bf16[1024,2,128]{2,0,1:T(8,128)(2,1)}, bf16[1024,2,128]{2,0,1:T(8,128)(2,1)S(1)}, u32[]{:S(2)}, u32[]{:S(2)}) %collective-permute-start) | collective-permute-done | bytes 524320 | tf_op jit(solution)/shard_map/while/body/eval_jaxpr/ppermute | solution.py:10
  72.7 5.5 %collective-permute-done.1 = bf16[1024,2,128]{0,2,1:T(8,128)(2,1)} collective-permute-done((bf16[1024,2,128]{0,2,1:T(8,128)(2,1)S(1)}, bf16[1024,2,128]{0,2,1:T(8,128)(2,1)}, u32[]{:S(2)}, u32[]{:S(2)}) %collective-permute-start.1) | collective-permute-done | bytes 524320 | tf_op jit(solution)/shard_map/while/body/eval_jaxpr/ppermute | solution.py:10
  78.3 13.0 %while.57 = (s32[]{:T(128)}, f32[1024,2,128]{0,2,1:T(8,128)}, s32[2]{0:T(128)S(1)}, bf16[1024,2,128]{0,2,1:T(8,128)(2,1)}, s32[24]{0:T(128)S(1)}, /*index=5*/s32...) while((s32[]{:T(128)}, f32[1024,2,128]{0,2,1:T(8,128)}, ...), condition=%wide.region_10.10_spmd, body=%wide.region_8.9_spmd.sunk | while | flops 546608128 | bytes 4215091 | solution.py:66
  80.2 4.6 %fusion.69 = f32[1024,2,128]{0,2,1:T(8,128)} fusion(f32[1024,2,128]{0,2,1:T(8,128)} %get-tuple-element.720, bf16[1024,2,128]{2,0,1:T(8,128)(2,1)} %get-tuple-element.742, pred[1024,512]{0,1:T(8,128)(4,1)S(1)} %and_and_fusion.5, bf16[1024,2,128]{2,0,1:T(8,128)(2,1)S(1)} %get-tuple-element.741, s32[]{:T(128)S(6)} %select_n.50, ...), kind=kOutput, calls=%fused_computation.12.clone.1 | convolution fusion | flops 544473088 | bytes 3671040 | tf_op jit(solution)/shard_map/while/body/eval_jaxpr/while/body/eval_jaxpr/hrk,khc->rhc/dot_general | solution.py:61
  86.7 4.6 %fusion.69 = f32[1024,2,128]{0,2,1:T(8,128)} fusion(f32[1024,2,128]{0,2,1:T(8,128)} %get-tuple-element.720, bf16[1024,2,128]{2,0,1:T(8,128)(2,1)} %get-tuple-element.742, pred[1024,512]{0,1:T(8,128)(4,1)S(1)} %and_and_fusion.5, bf16[1024,2,128]{2,0,1:T(8,128)(2,1)S(1)} %get-tuple-element.741, s32[]{:T(128)S(6)} %select_n.50, ...), kind=kOutput, calls=%fused_computation.12.clone.1 | convolution fusion | flops 544473088 | bytes 3671040 | tf_op jit(solution)/shard_map/while/body/eval_jaxpr/while/body/eval_jaxpr/hrk,khc->rhc/dot_general | solution.py:61
  93.1 1.6 copy.38
  94.7 1.3 reduce_sum.66
  96.7 2.4 %multiply_convert_fusion.2 = bf16[1024,2,128]{2,0,1:T(8,128)(2,1)} fusion(f32[1024,2,128]{2,0,1:T(8,128)S(1)} %copy.38, bf16[1024,2,512]{2,0,1:T(8,128)(2,1)} %copy-done.2, f32[2,128]{1,0:T(2,128)S(1)} %copy-done.3, f32[1024,2]{0,1:T(2,128)S(1)} %add_rsqrt_fusion, f32[1024,2]{0,1:T(2,128)S(1)} %broadcast_multiply_fusion), kind=kLoop, calls=%fused_computation.57 | loop fusion | flops 1572864 | bytes 2114560 | tf_op jit(solution)/shard_map/convert_element_type | solution.py:91
  99.0 2.0 %copy.39 = bf16[2,128,1024]{1,0,2:T(2,128)(2,1)} copy(bf16[2,128,1024]{2,1,0:T(8,128)(2,1)} %param.17) | data formatting | bytes 1048576 | tf_op args[5]
  101.1 4.6 %all-to-all-start = ((bf16[2,128,1024]{1,0,2:T(2,128)(2,1)}), bf16[2,128,1024]{1,0,2:T(2,128)(2,1)S(1)}, u32[]{:S(2)}, u32[]{:S(2)}) async-start(bf16[2,128,1024]{1,0,2:T(2,128)(2,1)} %copy.39), calls=%async_computation | async-start | bytes 1048576 | tf_op jit(solution)/shard_map/all_to_all | solution.py:92
  105.7 4.0 %convert_element_type.33 = f32[1024,1024]{1,0:T(8,128)} convert(bf16[1024,1024]{1,0:T(8,128)(2,1)} %param.12) | non-fusion elementwise | flops 1048576 | bytes 6291456 | tf_op jit(solution)/shard_map/convert_element_type | solution.py:21
  109.6 17.5 %all-to-all-done = bf16[2,128,1024]{1,0,2:T(2,128)(2,1)S(1)} async-done(((bf16[2,128,1024]{1,0,2:T(2,128)(2,1)}), bf16[2,128,1024]{1,0,2:T(2,128)(2,1)S(1)}, u32[]{:S(2)}, u32[]{:S(2)}) %all-to-all-start) | async-done | bytes 524320 | tf_op jit(solution)/shard_map/all_to_all | solution.py:92
  127.5 27.4 %all-gather.2.cloned.1.call-done = bf16[1024,8,128]{2,0,1:T(8,128)(2,1)} async-done(((bf16[1024,2,128]{2,0,1:T(8,128)(2,1)}), bf16[1024,8,128]{2,0,1:T(8,128)(2,1)}) %all-gather.2.cloned.1.call-update) | async-done | bytes 2097168 | tf_op jit(solution)/shard_map/all_gather | solution.py:95
  154.9 3.4 %fusion.48 = bf16[1024,256]{1,0:T(8,128)(2,1)} fusion(bf16[1024,8,128]{2,0,1:T(8,128)(2,1)} %all-gather.2.cloned.1.call-done, bf16[8,128,256]{2,1,0:T(8,128)(2,1)S(1)} %bitcast.89, f32[1024,1024]{1,0:T(8,128)} %convert_element_type.33, s32[]{:T(128)S(6)} %select_n.18), kind=kOutput, calls=%fused_computation.56 | convolution fusion | flops 537395200 | bytes 4194308 | tf_op jit(solution)/shard_map/rhc,hcd->rd/dot_general | solution.py:93
  (67 shorter events, 13.0 us)
Async XLA Ops:
  6.5 4.4 %copy-start = (bf16[1024,2,512]{2,1,0:T(2,128)(2,1)S(1)}, bf16[1024,2,512]{2,1,0:T(2,128)(2,1)}, u32[]{:S(2)}) copy-start(bf16[1024,2,512]{2,1,0:T(2,128)(2,1)} %param.15) | copy-start | bytes 6291460
  6.5 4.4 %copy-start.5 = (f32[1024]{0:T(1024)S(1)}, f32[1024]{0:T(1024)}, u32[]{:S(2)}) copy-start(f32[1024]{0:T(1024)} %param.14) | copy-start | bytes 12292
  6.5 148.4 %all-gather.2.cloned.1.call-start = ((), (), s32[]{:S(2)}) async-start(), calls=%async_computation.1 | async-start | bytes 2621440 | tf_op jit(solution)/shard_map/all_gather | solution.py:95
  6.5 4.4 %copy-start.1 = (bf16[1024,1024]{1,0:T(8,128)(2,1)S(1)}, bf16[1024,1024]{1,0:T(8,128)(2,1)}, u32[]{:S(2)}) copy-start(bf16[1024,1024]{1,0:T(8,128)(2,1)} %param.12) | copy-start | bytes 6291460
  14.4 1.4 copy-start.2
  15.7 1.5 copy-start.4
  30.5 10.1 %collective-permute-start = (bf16[1024,2,128]{2,0,1:T(8,128)(2,1)}, bf16[1024,2,128]{2,0,1:T(8,128)(2,1)S(1)}, u32[]{:S(2)}, u32[]{:S(2)}) collective-permute-start(bf16[1024,2,128]{2,0,1:T(8,128)(2,1)} %get-tuple-element.802), channel_id=1, source_target_pairs={{0,4},{4,8},{8,12},{12,16},{16,20},{20,24},{24,28},{1,5},{5,9},{9,... | collective-permute-start | bytes 1572872 | tf_op jit(solution)/shard_map/while/body/eval_jaxpr/ppermute | solution.py:10
  34.2 11.9 %collective-permute-start.1 = (bf16[1024,2,128]{0,2,1:T(8,128)(2,1)S(1)}, bf16[1024,2,128]{0,2,1:T(8,128)(2,1)}, u32[]{:S(2)}, u32[]{:S(2)}) collective-permute-start(bf16[1024,2,128]{0,2,1:T(8,128)(2,1)S(1)} %get-tuple-element.803), channel_id=1, source_target_pairs={{0,4},{4,8},{8,12},{12,16},{16,20},{20,24},{24,28},{1,5},{5,9},{9,... | collective-permute-start | bytes 1572872 | tf_op jit(solution)/shard_map/while/body/eval_jaxpr/ppermute | solution.py:10
  60.9 11.8 %collective-permute-start = (bf16[1024,2,128]{2,0,1:T(8,128)(2,1)}, bf16[1024,2,128]{2,0,1:T(8,128)(2,1)S(1)}, u32[]{:S(2)}, u32[]{:S(2)}) collective-permute-start(bf16[1024,2,128]{2,0,1:T(8,128)(2,1)} %get-tuple-element.802), channel_id=1, source_target_pairs={{0,4},{4,8},{8,12},{12,16},{16,20},{20,24},{24,28},{1,5},{5,9},{9,... | collective-permute-start | bytes 1572872 | tf_op jit(solution)/shard_map/while/body/eval_jaxpr/ppermute | solution.py:10
  66.3 11.9 %collective-permute-start.1 = (bf16[1024,2,128]{0,2,1:T(8,128)(2,1)S(1)}, bf16[1024,2,128]{0,2,1:T(8,128)(2,1)}, u32[]{:S(2)}, u32[]{:S(2)}) collective-permute-start(bf16[1024,2,128]{0,2,1:T(8,128)(2,1)S(1)} %get-tuple-element.803), channel_id=1, source_target_pairs={{0,4},{4,8},{8,12},{12,16},{16,20},{20,24},{24,28},{1,5},{5,9},{9,... | collective-permute-start | bytes 1572872 | tf_op jit(solution)/shard_map/while/body/eval_jaxpr/ppermute | solution.py:10
  93.1 3.6 %copy-start.3 = (f32[2,128]{1,0:T(2,128)S(1)}, f32[2,128]{1,0:T(2,128)}, u32[]{:S(2)}) copy-start(f32[2,128]{1,0:T(2,128)} %param.16) | copy-start | bytes 3076
  101.1 26.1 %all-to-all-start = ((bf16[2,128,1024]{1,0,2:T(2,128)(2,1)}), bf16[2,128,1024]{1,0,2:T(2,128)(2,1)S(1)}, u32[]{:S(2)}, u32[]{:S(2)}) async-start(bf16[2,128,1024]{1,0,2:T(2,128)(2,1)} %copy.39), calls=%async_computation | async-start | bytes 1048576 | tf_op jit(solution)/shard_map/all_to_all | solution.py:92
Sparse Core Ops, SparseCore 0:
  99.2 55.7 all-gather.1
where the time goes:
time: 166 us; the launch traced here: 165 us
  waiting for transfers between devices  64.9 us (39%)
  matrix products  33.8 us (20%)
  starting transfers between devices  17.5 us (11%)
  other arithmetic  16.9 us (10%)
  local copies, waits for them, and re-layouts  14.2 us (9%)
  between operations  13.5 us (8%)
  loops' own time  4.27 us (3%)
    all_gather x1, waiting for transfers between devices, on_device(): lax.all_gather(gated, 'narrow', axis=1, tiled=True)  27.4 us
    dot_general x6, matrix products, block_step(): jnp.einsum('hrk,khc->rhc', weights, value_block, preferred_element_type=j...  27.1 us
    ppermute x4, waiting for transfers between devices, from_behind(): lax.ppermute(value, axis, [(source, source + steps) for source in range(i...  20 us
    all_to_all x1, waiting for transfers between devices, on_device(): lax.all_to_all(w_out, 'narrow', split_axis=2, concat_axis=0, tiled=True)  17.5 us
    ppermute x4, starting transfers between devices, from_behind(): lax.ppermute(value, axis, [(source, source + steps) for source in range(i...  12.9 us
    all_to_all x1, starting transfers between devices, on_device(): lax.all_to_all(w_out, 'narrow', split_axis=2, concat_axis=0, tiled=True)  4.59 us
    another operation x3, loops' own time, attend(): lax.scan(block_step, running, jnp.arange(key_count // block_rows, dtype=j...  4.21 us
    convert_element_type x1, other arithmetic, on_device(): events_f = events.astype(jnp.float32)  3.98 us
  transfers between devices with their start and end apart: 6, of which 6 were waited for; matrix products, arithmetic and copies ran while one was open for 4% of the time, Pallas kernels for 0%

commit v1 on v0

--- a/solution.py
+++ b/solution.py
@@ -2,6 +2,28 @@
 import jax.numpy as jnp
 from jax import lax
 from jax.sharding import PartitionSpec as P
+
+
+def laid_out(blocks, dim):
+    shape = list(blocks.shape[1:])
+    shape[dim] *= blocks.shape[0]
+    return jnp.moveaxis(blocks, 0, dim).reshape(shape)
+
+
+def ring_gather(x, axis, dim):
+    count = lax.axis_size(axis)
+    pairs = [(i, (i + 1) % count) for i in range(count)]
+    back = [(b, a) for a, b in pairs]
+    lower, upper = ([], [])
+    for turn in range(count - 1):
+        if turn % 2 == 0:
+            lower.append(lax.ppermute(lower[-1] if lower else x, axis, pairs))
+        else:
+            upper.append(lax.ppermute(upper[-1] if upper else x, axis, back))
+    tiles = jnp.stack([*lower[::-1], x, *upper])
+    shift = lax.axis_index(axis) - len(lower)
+    tiles = tiles[(jnp.arange(count) - shift) % count]
+    return laid_out(tiles, dim)
 
 
 def from_behind(value, axis, steps):
@@ -91,10 +113,7 @@
     gated = gated.astype(jnp.bfloat16)
     columns = lax.all_to_all(w_out, "narrow", split_axis=2, concat_axis=0, tiled=True)
     summed = jnp.einsum(
-        "rhc,hcd->rd",
-        lax.all_gather(gated, "narrow", axis=1, tiled=True),
-        columns,
-        preferred_element_type=jnp.float32,
+        "rhc,hcd->rd", ring_gather(gated, "narrow", 1), columns, preferred_element_type=jnp.float32
     )
     share = summed.shape[1]
     own_cols = lax.dynamic_slice_in_dim(events_f, lax.axis_index("narrow") * share, share, 1)

time: 166 us -> 151 us (0.910)
  the two profiles are of different devices: /device:TPU:3 before, /device:TPU:11 now
where the time goes in v1:
time: 151 us; the launch traced here: 150 us
  waiting for transfers between devices  55.9 us (37%)
  matrix products  33.7 us (22%)
  starting transfers between devices  19.3 us (13%)
  other arithmetic  18.5 us (12%)
  local copies, waits for them, and re-layouts  18.2 us (12%)
  loops' own time  4.28 us (3%)
    dot_general x6, matrix products, block_step(): jnp.einsum('hrk,khc->rhc', weights, value_block, preferred_element_type=j...  27 us
    ppermute x4, waiting for transfers between devices, from_behind(): lax.ppermute(value, axis, [(source, source + steps) for source in range(i...  20 us
    all_to_all x1, waiting for transfers between devices, on_device(): lax.all_to_all(w_out, 'narrow', split_axis=2, concat_axis=0, tiled=True)  16.3 us
    ppermute x1, waiting for transfers between devices, ring_gather(): upper.append(lax.ppermute(upper[-1] if upper else x, axis, back))  13.5 us
    ppermute x4, starting transfers between devices, from_behind(): lax.ppermute(value, axis, [(source, source + steps) for source in range(i...  12.9 us
    ppermute x2, waiting for transfers between devices, ring_gather(): lower.append(lax.ppermute(lower[-1] if lower else x, axis, pairs))  6.14 us
    another operation x3, loops' own time, attend(): lax.scan(block_step, running, jnp.arange(key_count // block_rows, dtype=j...  4.21 us
    convert_element_type x1, other arithmetic, on_device(): events_f = events.astype(jnp.float32)  3.98 us
  transfers between devices with their start and end apart: 8, of which 7 were waited for; matrix products, arithmetic and copies ran while one was open for 4% of the time, Pallas kernels for 0%

profile of v1, /device:TPU:11, one launch (start us, length us, event | category | flops | bytes accessed | tf_op | source)
XLA Modules:
  0.0 150.0 jit_solution(9890938253040858357)
XLA Ops:
  0.0 2.1 %convert_reduce_fusion.2 = f32[1024]{0:T(1024)S(1)} fusion(bf16[1024,1024]{1,0:T(8,128)(2,1)} %param.12), kind=kLoop, calls=%fused_computation.48 | loop fusion | flops 2096128 | bytes 2101248 | tf_op jit(solution)/shard_map/reduce_sum | solution.py:44
  3.1 3.4 %multiply_convert_fusion = bf16[1024,2,512]{2,0,1:T(8,128)(2,1)S(1)} fusion(bf16[1024,2,512]{2,1,0:T(2,128)(2,1)S(1)} %copy-done, bf16[1024,1024]{1,0:T(8,128)(2,1)S(1)} %copy-done.1, f32[1024]{0:T(1024)S(1)} %copy-done.5, f32[1024]{0:T(1024)S(1)} %add_rsqrt_fusion.1, f32[1024]{0:T(1024)S(1)} %broadcast_multiply_fusion.1), kind=kOutput, calls=%fused_computation.45 | convolution fusion | flops 2157969408 | bytes 6303744 | tf_op jit(solution)/shard_map/rd,dhc->rhc/dot_general | solution.py:47
  9.7 12.9 %while.56 = (s32[]{:T(128)}, f32[1024,2,128]{0,2,1:T(8,128)}, s32[2]{0:T(128)S(1)}, bf16[1024,2,128]{0,2,1:T(8,128)(2,1)S(1)}, s32[24]{0:T(128)S(1)}, /*index=5*...) while((s32[]{:T(128)}, f32[1024,2,128]{0,2,1:T(8,128)}, ...), condition=%wide.region_6.7_spmd.clone.clone.clone, body=%wide.region_4.6_spmd.clone.clone.clone.sunk | while | flops 546871296 | bytes 4219704 | solution.py:88
  11.8 4.2 %fusion.67 = f32[1024,2,128]{0,2,1:T(8,128)} fusion(bf16[1024,2,128]{2,0,1:T(8,128)(2,1)} %get-tuple-element.781, pred[1024,512]{0,1:T(8,128)(4,1)S(1)} %and_and_fusion.4, f32[1024,2,128]{0,2,1:T(8,128)} %get-tuple-element.761, pred[]{:T(512)S(6)} %compare.12, bf16[1024,2,128]{2,0,1:T(8,128)(2,1)} %get-tuple-element.780, s32[]{:T(128)S(6)} %select_n.82, ...), kind=kOutput, calls=%fused_computation.34.clone.1 | convolution fusion | flops 544735232 | bytes 3671552 | tf_op jit(solution)/shard_map/while/body/eval_jaxpr/hrk,khc->rhc/dot_general | solution.py:83
  18.0 4.6 %fusion.67 = f32[1024,2,128]{0,2,1:T(8,128)} fusion(bf16[1024,2,128]{2,0,1:T(8,128)(2,1)} %get-tuple-element.781, pred[1024,512]{0,1:T(8,128)(4,1)S(1)} %and_and_fusion.4, f32[1024,2,128]{0,2,1:T(8,128)} %get-tuple-element.761, pred[]{:T(512)S(6)} %compare.12, bf16[1024,2,128]{2,0,1:T(8,128)(2,1)} %get-tuple-element.780, s32[]{:T(128)S(6)} %select_n.82, ...), kind=kOutput, calls=%fused_computation.34.clone.1 | convolution fusion | flops 544735232 | bytes 3671552 | tf_op jit(solution)/shard_map/while/body/eval_jaxpr/hrk,khc->rhc/dot_general | solution.py:83
  22.6 62.5 %while.55 = (s32[]{:T(128)}, bf16[1024,2,128]{2,0,1:T(8,128)(2,1)}, bf16[1024,2,128]{0,2,1:T(8,128)(2,1)S(1)}, f32[1024,2,128]{0,2,1:T(8,128)}, s32[]{:T(128)}, ...) while((s32[]{:T(128)}, bf16[1024,2,128]{2,0,1:T(8,128)(2,1)}, ...), condition=%wide.region_11.12_spmd.clone.clone, body=%wide.region_7.11_spmd.clone.clone.sunk | while | flops 546609152 | bytes 10511020 | solution.py:104
  22.6 3.7 %collective-permute-start = (bf16[1024,2,128]{2,0,1:T(8,128)(2,1)}, bf16[1024,2,128]{2,0,1:T(8,128)(2,1)S(1)}, u32[]{:S(2)}, u32[]{:S(2)}) collective-permute-start(bf16[1024,2,128]{2,0,1:T(8,128)(2,1)} %get-tuple-element.802), channel_id=1, source_target_pairs={{0,4},{4,8},{8,12},{12,16},{16,20},{20,24},{24,28},{1,5},{5,9},{9,... | collective-permute-start | bytes 1572872 | tf_op jit(solution)/shard_map/while/body/eval_jaxpr/ppermute | solution.py:32
  26.3 1.9 %collective-permute-start.1 = (bf16[1024,2,128]{0,2,1:T(8,128)(2,1)S(1)}, bf16[1024,2,128]{0,2,1:T(8,128)(2,1)}, u32[]{:S(2)}, u32[]{:S(2)}) collective-permute-start(bf16[1024,2,128]{0,2,1:T(8,128)(2,1)S(1)} %get-tuple-element.803), channel_id=1, source_target_pairs={{0,4},{4,8},{8,12},{12,16},{16,20},{20,24},{24,28},{1,5},{5,9},{9,... | collective-permute-start | bytes 1572872 | tf_op jit(solution)/shard_map/while/body/eval_jaxpr/ppermute | solution.py:32
  28.2 4.5 %collective-permute-done = bf16[1024,2,128]{2,0,1:T(8,128)(2,1)S(1)} collective-permute-done((bf16[1024,2,128]{2,0,1:T(8,128)(2,1)}, bf16[1024,2,128]{2,0,1:T(8,128)(2,1)S(1)}, u32[]{:S(2)}, u32[]{:S(2)}) %collective-permute-start) | collective-permute-done | bytes 524320 | tf_op jit(solution)/shard_map/while/body/eval_jaxpr/ppermute | solution.py:32
  32.7 5.5 %collective-permute-done.1 = bf16[1024,2,128]{0,2,1:T(8,128)(2,1)} collective-permute-done((bf16[1024,2,128]{0,2,1:T(8,128)(2,1)S(1)}, bf16[1024,2,128]{0,2,1:T(8,128)(2,1)}, u32[]{:S(2)}, u32[]{:S(2)}) %collective-permute-start.1) | collective-permute-done | bytes 524320 | tf_op jit(solution)/shard_map/while/body/eval_jaxpr/ppermute | solution.py:32
  38.2 13.0 %while.57 = (s32[]{:T(128)}, f32[1024,2,128]{0,2,1:T(8,128)}, s32[2]{0:T(128)S(1)}, bf16[1024,2,128]{0,2,1:T(8,128)(2,1)}, s32[24]{0:T(128)S(1)}, /*index=5*/s32...) while((s32[]{:T(128)}, f32[1024,2,128]{0,2,1:T(8,128)}, ...), condition=%wide.region_10.10_spmd, body=%wide.region_8.9_spmd.sunk | while | flops 546608128 | bytes 4215091 | solution.py:88
  40.1 4.6 %fusion.71 = f32[1024,2,128]{0,2,1:T(8,128)} fusion(f32[1024,2,128]{0,2,1:T(8,128)} %get-tuple-element.720, bf16[1024,2,128]{2,0,1:T(8,128)(2,1)} %get-tuple-element.742, pred[1024,512]{0,1:T(8,128)(4,1)S(1)} %and_and_fusion.5, bf16[1024,2,128]{2,0,1:T(8,128)(2,1)S(1)} %get-tuple-element.741, s32[]{:T(128)S(6)} %select_n.84, ...), kind=kOutput, calls=%fused_computation.13.clone.1 | convolution fusion | flops 544473088 | bytes 3671040 | tf_op jit(solution)/shard_map/while/body/eval_jaxpr/while/body/eval_jaxpr/hrk,khc->rhc/dot_general | solution.py:83
  46.6 4.6 %fusion.71 = f32[1024,2,128]{0,2,1:T(8,128)} fusion(f32[1024,2,128]{0,2,1:T(8,128)} %get-tuple-element.720, bf16[1024,2,128]{2,0,1:T(8,128)(2,1)} %get-tuple-element.742, pred[1024,512]{0,1:T(8,128)(4,1)S(1)} %and_and_fusion.5, bf16[1024,2,128]{2,0,1:T(8,128)(2,1)S(1)} %get-tuple-element.741, s32[]{:T(128)S(6)} %select_n.84, ...), kind=kOutput, calls=%fused_computation.13.clone.1 | convolution fusion | flops 544473088 | bytes 3671040 | tf_op jit(solution)/shard_map/while/body/eval_jaxpr/while/body/eval_jaxpr/hrk,khc->rhc/dot_general | solution.py:83
  53.0 5.4 %collective-permute-start = (bf16[1024,2,128]{2,0,1:T(8,128)(2,1)}, bf16[1024,2,128]{2,0,1:T(8,128)(2,1)S(1)}, u32[]{:S(2)}, u32[]{:S(2)}) collective-permute-start(bf16[1024,2,128]{2,0,1:T(8,128)(2,1)} %get-tuple-element.802), channel_id=1, source_target_pairs={{0,4},{4,8},{8,12},{12,16},{16,20},{20,24},{24,28},{1,5},{5,9},{9,... | collective-permute-start | bytes 1572872 | tf_op jit(solution)/shard_map/while/body/eval_jaxpr/ppermute | solution.py:32
  58.4 1.9 %collective-permute-start.1 = (bf16[1024,2,128]{0,2,1:T(8,128)(2,1)S(1)}, bf16[1024,2,128]{0,2,1:T(8,128)(2,1)}, u32[]{:S(2)}, u32[]{:S(2)}) collective-permute-start(bf16[1024,2,128]{0,2,1:T(8,128)(2,1)S(1)} %get-tuple-element.803), channel_id=1, source_target_pairs={{0,4},{4,8},{8,12},{12,16},{16,20},{20,24},{24,28},{1,5},{5,9},{9,... | collective-permute-start | bytes 1572872 | tf_op jit(solution)/shard_map/while/body/eval_jaxpr/ppermute | solution.py:32
  60.3 4.5 %collective-permute-done = bf16[1024,2,128]{2,0,1:T(8,128)(2,1)S(1)} collective-permute-done((bf16[1024,2,128]{2,0,1:T(8,128)(2,1)}, bf16[1024,2,128]{2,0,1:T(8,128)(2,1)S(1)}, u32[]{:S(2)}, u32[]{:S(2)}) %collective-permute-start) | collective-permute-done | bytes 524320 | tf_op jit(solution)/shard_map/while/body/eval_jaxpr/ppermute | solution.py:32
  64.8 5.5 %collective-permute-done.1 = bf16[1024,2,128]{0,2,1:T(8,128)(2,1)} collective-permute-done((bf16[1024,2,128]{0,2,1:T(8,128)(2,1)S(1)}, bf16[1024,2,128]{0,2,1:T(8,128)(2,1)}, u32[]{:S(2)}, u32[]{:S(2)}) %collective-permute-start.1) | collective-permute-done | bytes 524320 | tf_op jit(solution)/shard_map/while/body/eval_jaxpr/ppermute | solution.py:32
  70.3 13.0 %while.57 = (s32[]{:T(128)}, f32[1024,2,128]{0,2,1:T(8,128)}, s32[2]{0:T(128)S(1)}, bf16[1024,2,128]{0,2,1:T(8,128)(2,1)}, s32[24]{0:T(128)S(1)}, /*index=5*/s32...) while((s32[]{:T(128)}, f32[1024,2,128]{0,2,1:T(8,128)}, ...), condition=%wide.region_10.10_spmd, body=%wide.region_8.9_spmd.sunk | while | flops 546608128 | bytes 4215091 | solution.py:88
  72.2 4.6 %fusion.71 = f32[1024,2,128]{0,2,1:T(8,128)} fusion(f32[1024,2,128]{0,2,1:T(8,128)} %get-tuple-element.720, bf16[1024,2,128]{2,0,1:T(8,128)(2,1)} %get-tuple-element.742, pred[1024,512]{0,1:T(8,128)(4,1)S(1)} %and_and_fusion.5, bf16[1024,2,128]{2,0,1:T(8,128)(2,1)S(1)} %get-tuple-element.741, s32[]{:T(128)S(6)} %select_n.84, ...), kind=kOutput, calls=%fused_computation.13.clone.1 | convolution fusion | flops 544473088 | bytes 3671040 | tf_op jit(solution)/shard_map/while/body/eval_jaxpr/while/body/eval_jaxpr/hrk,khc->rhc/dot_general | solution.py:83
  78.7 4.6 %fusion.71 = f32[1024,2,128]{0,2,1:T(8,128)} fusion(f32[1024,2,128]{0,2,1:T(8,128)} %get-tuple-element.720, bf16[1024,2,128]{2,0,1:T(8,128)(2,1)} %get-tuple-element.742, pred[1024,512]{0,1:T(8,128)(4,1)S(1)} %and_and_fusion.5, bf16[1024,2,128]{2,0,1:T(8,128)(2,1)S(1)} %get-tuple-element.741, s32[]{:T(128)S(6)} %select_n.84, ...), kind=kOutput, calls=%fused_computation.13.clone.1 | convolution fusion | flops 544473088 | bytes 3671040 | tf_op jit(solution)/shard_map/while/body/eval_jaxpr/while/body/eval_jaxpr/hrk,khc->rhc/dot_general | solution.py:83
  85.1 1.6 %copy.38 = f32[1024,2,128]{2,0,1:T(8,128)S(1)} copy(f32[1024,2,128]{0,2,1:T(8,128)} %get-tuple-element.266) | data formatting | bytes 2097152 | tf_op jit(solution)/shard_map/while | solution.py:104
  88.7 2.4 %multiply_convert_fusion.2 = bf16[1024,2,128]{2,0,1:T(8,128)(2,1)} fusion(f32[1024,2,128]{2,0,1:T(8,128)S(1)} %copy.38, bf16[1024,2,512]{2,0,1:T(8,128)(2,1)} %copy-done.2, f32[2,128]{1,0:T(2,128)S(1)} %copy-done.3, f32[1024,2]{0,1:T(2,128)S(1)} %add_rsqrt_fusion, f32[1024,2]{0,1:T(2,128)S(1)} %broadcast_multiply_fusion), kind=kLoop, calls=%fused_computation.59 | loop fusion | flops 1572864 | bytes 2114560 | tf_op jit(solution)/shard_map/convert_element_type | solution.py:113
  92.4 2.0 %copy.39 = bf16[2,128,1024]{1,0,2:T(2,128)(2,1)} copy(bf16[2,128,1024]{2,1,0:T(8,128)(2,1)} %param.17) | data formatting | bytes 1048576 | tf_op args[5]
  94.4 3.7 %all-to-all-start = ((bf16[2,128,1024]{1,0,2:T(2,128)(2,1)}), bf16[2,128,1024]{1,0,2:T(2,128)(2,1)S(1)}, u32[]{:S(2)}, u32[]{:S(2)}) async-start(bf16[2,128,1024]{1,0,2:T(2,128)(2,1)} %copy.39), calls=%async_computation | async-start | bytes 1048576 | tf_op jit(solution)/shard_map/all_to_all | solution.py:114
  98.1 6.1 %collective-permute-done.2 = bf16[1024,2,128]{2,0,1:T(8,128)(2,1)} collective-permute-done((bf16[1024,2,128]{2,0,1:T(8,128)(2,1)}, bf16[1024,2,128]{2,0,1:T(8,128)(2,1)}, u32[]{:S(2)}, u32[]{:S(2)}) %collective-permute-start.2) | collective-permute-done | bytes 524320 | tf_op jit(solution)/shard_map/ppermute | solution.py:20
  104.2 1.3 collective-permute-start.3
  105.6 4.0 %convert_element_type.33 = f32[1024,1024]{1,0:T(8,128)} convert(bf16[1024,1024]{1,0:T(8,128)(2,1)} %param.12) | non-fusion elementwise | flops 1048576 | bytes 6291456 | tf_op jit(solution)/shard_map/convert_element_type | solution.py:43
  109.6 16.3 %all-to-all-done = bf16[2,128,1024]{1,0,2:T(2,128)(2,1)S(1)} async-done(((bf16[2,128,1024]{1,0,2:T(2,128)(2,1)}), bf16[2,128,1024]{1,0,2:T(2,128)(2,1)S(1)}, u32[]{:S(2)}, u32[]{:S(2)}) %all-to-all-start) | async-done | bytes 524320 | tf_op jit(solution)/shard_map/all_to_all | solution.py:114
  126.3 13.5 %collective-permute-done.4 = bf16[1024,2,128]{2,0,1:T(8,128)(2,1)} collective-permute-done((bf16[1024,2,128]{2,0,1:T(8,128)(2,1)}, bf16[1024,2,128]{2,0,1:T(8,128)(2,1)}, u32[]{:S(2)}, u32[]{:S(2)}) %collective-permute-start.4) | collective-permute-done | bytes 524320 | tf_op jit(solution)/shard_map/ppermute | solution.py:22
  139.8 3.1 %pad_maximum_fusion = bf16[4,1024,2,128]{3,1,2,0:T(8,128)(2,1)} fusion(bf16[1,1024,2,128]{3,1,2,0:T(8,128)(2,1)} %bitcast.8, bf16[1,1024,2,128]{3,1,2,0:T(8,128)(2,1)} %bitcast.7, bf16[1,1024,2,128]{3,1,2,0:T(8,128)(2,1)} %bitcast.6, bf16[1,1024,2,128]{3,1,2,0:T(8,128)(2,1)} %bitcast.5), kind=kLoop, calls=%fused_computation.51 | loop fusion | flops 3145728 | bytes 4194304 | tf_op jit(solution)/shard_map/stack | solution.py:23
  142.9 3.7 %gather_fusion = bf16[4,1024,2,128]{3,1,2,0:T(8,128)(2,1)} fusion(bf16[4,1024,2,128]{3,1,2,0:T(8,128)(2,1)} %pad_maximum_fusion, s32[1024]{0:T(1024)S(1)} %pad_clamp_fusion), kind=kCustom, calls=%fused_computation | custom fusion | bytes 4194320 | tf_op jit(solution)/shard_map/gather | solution.py:25
  146.6 3.4 %fusion.48 = bf16[1024,256]{1,0:T(8,128)(2,1)} fusion(bf16[1024,8,128]{2,0,1:T(8,128)(2,1)} %bitcast.97, bf16[8,128,256]{2,1,0:T(8,128)(2,1)S(1)} %bitcast.99, f32[1024,1024]{1,0:T(8,128)} %convert_element_type.33, s32[]{:T(128)S(6)} %select_n.42), kind=kOutput, calls=%fused_computation.58 | convolution fusion | flops 537395200 | bytes 4194308 | tf_op jit(solution)/shard_map/rhc,hcd->rd/dot_general | solution.py:115
  (74 shorter events, 19.1 us)
Async XLA Ops:
  0.0 3.1 %copy-start = (bf16[1024,2,512]{2,1,0:T(2,128)(2,1)S(1)}, bf16[1024,2,512]{2,1,0:T(2,128)(2,1)}, u32[]{:S(2)}) copy-start(bf16[1024,2,512]{2,1,0:T(2,128)(2,1)} %param.15) | copy-start | bytes 6291460
  0.0 2.4 %copy-start.1 = (bf16[1024,1024]{1,0:T(8,128)(2,1)S(1)}, bf16[1024,1024]{1,0:T(8,128)(2,1)}, u32[]{:S(2)}) copy-start(bf16[1024,1024]{1,0:T(8,128)(2,1)} %param.12) | copy-start | bytes 6291460
  0.0 3.1 %copy-start.5 = (f32[1024]{0:T(1024)S(1)}, f32[1024]{0:T(1024)}, u32[]{:S(2)}) copy-start(f32[1024]{0:T(1024)} %param.14) | copy-start | bytes 12292
  6.5 1.4 copy-start.2
  7.8 1.5 copy-start.4
  22.6 10.1 %collective-permute-start = (bf16[1024,2,128]{2,0,1:T(8,128)(2,1)}, bf16[1024,2,128]{2,0,1:T(8,128)(2,1)S(1)}, u32[]{:S(2)}, u32[]{:S(2)}) collective-permute-start(bf16[1024,2,128]{2,0,1:T(8,128)(2,1)} %get-tuple-element.802), channel_id=1, source_target_pairs={{0,4},{4,8},{8,12},{12,16},{16,20},{20,24},{24,28},{1,5},{5,9},{9,... | collective-permute-start | bytes 1572872 | tf_op jit(solution)/shard_map/while/body/eval_jaxpr/ppermute | solution.py:32
  26.3 11.9 %collective-permute-start.1 = (bf16[1024,2,128]{0,2,1:T(8,128)(2,1)S(1)}, bf16[1024,2,128]{0,2,1:T(8,128)(2,1)}, u32[]{:S(2)}, u32[]{:S(2)}) collective-permute-start(bf16[1024,2,128]{0,2,1:T(8,128)(2,1)S(1)} %get-tuple-element.803), channel_id=1, source_target_pairs={{0,4},{4,8},{8,12},{12,16},{16,20},{20,24},{24,28},{1,5},{5,9},{9,... | collective-permute-start | bytes 1572872 | tf_op jit(solution)/shard_map/while/body/eval_jaxpr/ppermute | solution.py:32
  53.0 11.8 %collective-permute-start = (bf16[1024,2,128]{2,0,1:T(8,128)(2,1)}, bf16[1024,2,128]{2,0,1:T(8,128)(2,1)S(1)}, u32[]{:S(2)}, u32[]{:S(2)}) collective-permute-start(bf16[1024,2,128]{2,0,1:T(8,128)(2,1)} %get-tuple-element.802), channel_id=1, source_target_pairs={{0,4},{4,8},{8,12},{12,16},{16,20},{20,24},{24,28},{1,5},{5,9},{9,... | collective-permute-start | bytes 1572872 | tf_op jit(solution)/shard_map/while/body/eval_jaxpr/ppermute | solution.py:32
  58.4 11.9 %collective-permute-start.1 = (bf16[1024,2,128]{0,2,1:T(8,128)(2,1)S(1)}, bf16[1024,2,128]{0,2,1:T(8,128)(2,1)}, u32[]{:S(2)}, u32[]{:S(2)}) collective-permute-start(bf16[1024,2,128]{0,2,1:T(8,128)(2,1)S(1)} %get-tuple-element.803), channel_id=1, source_target_pairs={{0,4},{4,8},{8,12},{12,16},{16,20},{20,24},{24,28},{1,5},{5,9},{9,... | collective-permute-start | bytes 1572872 | tf_op jit(solution)/shard_map/while/body/eval_jaxpr/ppermute | solution.py:32
  85.1 3.6 %copy-start.3 = (f32[2,128]{1,0:T(2,128)S(1)}, f32[2,128]{1,0:T(2,128)}, u32[]{:S(2)}) copy-start(f32[2,128]{1,0:T(2,128)} %param.16) | copy-start | bytes 3076
  91.0 13.2 %collective-permute-start.2 = (bf16[1024,2,128]{2,0,1:T(8,128)(2,1)}, bf16[1024,2,128]{2,0,1:T(8,128)(2,1)}, u32[]{:S(2)}, u32[]{:S(2)}) collective-permute-start(bf16[1024,2,128]{2,0,1:T(8,128)(2,1)} %multiply_convert_fusion.2), channel_id=1, source_target_pairs={{0,1},{1,2},{2,3},{3,0},{4,5},{5,6},{6,7},{7,4},{8,9},{9,10},{10,1... | collective-permute-start | bytes 1572872 | tf_op jit(solution)/shard_map/ppermute | solution.py:20
  94.4 31.5 %all-to-all-start = ((bf16[2,128,1024]{1,0,2:T(2,128)(2,1)}), bf16[2,128,1024]{1,0,2:T(2,128)(2,1)S(1)}, u32[]{:S(2)}, u32[]{:S(2)}) async-start(bf16[2,128,1024]{1,0,2:T(2,128)(2,1)} %copy.39), calls=%async_computation | async-start | bytes 1048576 | tf_op jit(solution)/shard_map/all_to_all | solution.py:114
  98.1 41.7 %collective-permute-start.4 = (bf16[1024,2,128]{2,0,1:T(8,128)(2,1)}, bf16[1024,2,128]{2,0,1:T(8,128)(2,1)}, u32[]{:S(2)}, u32[]{:S(2)}) collective-permute-start(bf16[1024,2,128]{2,0,1:T(8,128)(2,1)} %multiply_convert_fusion.2), channel_id=1, source_target_pairs={{1,0},{2,1},{3,2},{0,3},{5,4},{6,5},{7,6},{4,7},{9,8},{10,9},{11,1... | collective-permute-start | bytes 1572872 | tf_op jit(solution)/shard_map/ppermute | solution.py:22
  104.2 35.6 %collective-permute-start.3 = (bf16[1024,2,128]{2,0,1:T(8,128)(2,1)}, bf16[1024,2,128]{2,0,1:T(8,128)(2,1)}, u32[]{:S(2)}, u32[]{:S(2)}) collective-permute-start(bf16[1024,2,128]{2,0,1:T(8,128)(2,1)} %collective-permute-done.2), channel_id=1, source_target_pairs={{0,1},{1,2},{2,3},{3,0},{4,5},{5,6},{6,7},{7,4},{8,9},{9,10},{10,1... | collective-permute-start | bytes 1572872 | tf_op jit(solution)/shard_map/ppermute | solution.py:20
